TPU v7x, 256 devices: a whole 4x4x8 slice. The times are simulated.
256 devices in a mesh: req: 16 (over y, x_hi, core), blk: 16 (over z, x_lo).
Axes of the slice: x: 4 (x_hi: 2, x_lo: 2; x = x_hi * 2 + x_lo), y: 4, z: 8, core: 2. Of those that a mesh axis runs over, the one named last changes fastest.
Arguments:
- tokens: bfloat16 [32, 256, 1600], P('req'), may hold values from -6 to 6
- cache_kv: bfloat16 [4, 8192, 16, 128], P(None, 'req', 'blk'), may hold values from -500 to 500
- w_qkv: bfloat16 [1600, 16, 192], P(None, 'blk'), may hold values from -0.15625 to 0.15625
- w_out: bfloat16 [16, 64, 1600], P('blk'), may hold values from -0.1875 to 0.1875
- w_fc: bfloat16 [1600, 6400], P(None, 'blk'), may hold values from -0.15625 to 0.15625
- w_proj: bfloat16 [6400, 1600], P('blk'), may hold values from -0.078125 to 0.078125
- embed_table: bfloat16 [50256, 1600], P('req', 'blk'), may hold values from -6 to 6
- group_ids: int32 [32], replicated, may hold values from 0 to 3, never falling along the last dimension, each value on 1 to 16 neighbouring positions
- cache_len: int32 [4], replicated, may hold values from 512 to 8192, as said below
- accept: int32 [2, 32, 256], P(None, 'req'), may hold values 0 or 1
- new_ids: int32 [2, 32, 256], replicated, may hold values from 0 to 50255
Outputs:
- denoised: bfloat16 [32, 256, 1600], P('req')
Inputs may be any that keep to these rules, and one draw needn't show every extreme that they name: `group_ids`: requests of one group stand in consecutive order; each of the 4 groups holds 1 to 16 requests and one holds exactly 16. Cache positions 0 to cache_len[g] - 1 of group g are live; one group's cache is full in every draw.
All inputs are finite; a program needn't handle non-finite values. No bound on the sum of `accept` on one device may be relied on, other than what follows from the above.
Results may differ from a plain program's by a relative error of at most 0.04.
Values may be sent and summed in bfloat16 or wider, within the bound.
A program may use at most 128 MiB of HBM per device.

v0:
```python
import jax
import jax.numpy as jnp
from jax import lax
from jax.sharding import PartitionSpec as P

PASSES = 2


def layer_norm(values):
    centre = values - jnp.mean(values, -1, keepdims=True)
    spread = jnp.mean(centre * centre, -1, keepdims=True)
    return centre * lax.rsqrt(spread + 1e-05)


def attend(projected, own_cache, lengths, head_dim):
    queries = projected[..., :head_dim]
    keys_new = projected[..., head_dim : 2 * head_dim]
    values_new = projected[..., 2 * head_dim :]
    factor = head_dim ** (-0.5)
    scores = (
        jnp.einsum("rqhd,rkhd->rhqk", queries, keys_new, preferred_element_type=jnp.float32)
        * factor
    )
    highest = jnp.max(scores, -1)
    weights_raw = jnp.exp(scores - highest[..., None])
    totals = jnp.sum(weights_raw, -1)
    gathered = jnp.einsum(
        "rhqk,rkhd->rhqd",
        weights_raw.astype(jnp.bfloat16),
        values_new,
        preferred_element_type=jnp.float32,
    )
    cache_size = own_cache.shape[1]
    key_span = min(1024, cache_size)

    def visit_block(block_index, carried):
        highest, totals, gathered = carried
        cache_piece = lax.dynamic_slice_in_dim(own_cache, block_index * key_span, key_span, 1)
        scores = (
            jnp.einsum(
                "rqhd,rkhd->rhqk",
                queries,
                cache_piece[..., :head_dim],
                preferred_element_type=jnp.float32,
            )
            * factor
        )
        position = block_index * key_span + jnp.arange(key_span, dtype=jnp.int32)
        scores = jnp.where(
            position[None, None, None, :] < lengths[:, None, None, None], scores, -1e30
        )
        raised = jnp.maximum(highest, jnp.max(scores, -1))
        shrink = jnp.exp(highest - raised)
        weights_raw = jnp.exp(scores - raised[..., None])
        totals = totals * shrink + jnp.sum(weights_raw, -1)
        gathered = gathered * shrink[..., None] + jnp.einsum(
            "rhqk,rkhd->rhqd",
            weights_raw.astype(jnp.bfloat16),
            cache_piece[..., head_dim:],
            preferred_element_type=jnp.float32,
        )
        return (raised, totals, gathered)

    highest, totals, gathered = lax.fori_loop(
        0, cache_size // key_span, visit_block, (highest, totals, gathered)
    )
    mixed_heads = gathered / totals[..., None]
    return jnp.transpose(mixed_heads, (0, 2, 1, 3)).astype(jnp.bfloat16)


def shards(
    tokens, cache_kv, w_qkv, w_out, w_fc, w_proj, embed_table, group_ids, cache_len, accept, new_ids
):
    req_index = lax.axis_index("req")
    per_device = tokens.shape[0]
    kv_width = cache_kv.shape[3]
    head_dim = kv_width // 2
    my_groups = lax.dynamic_slice_in_dim(group_ids, req_index * per_device, per_device)
    every_cache = lax.all_gather(cache_kv, "req", axis=1, tiled=True)
    own_cache = jnp.take(every_cache, my_groups, axis=0)
    lengths = jnp.take(cache_len, my_groups)
    vocab_dev = embed_table.shape[0]
    relative = new_ids - req_index * vocab_dev
    inside = (relative >= 0) & (relative < vocab_dev)
    looked = jnp.take(embed_table, jnp.clip(relative, 0, vocab_dev - 1), axis=0)
    looked = jnp.where(inside[..., None], looked, jnp.zeros((), jnp.bfloat16))
    picked = (
        lax.psum_scatter(looked, "req", scatter_dimension=1, tiled=True)
        .astype(jnp.float32)
        .astype(jnp.bfloat16)
    )
    fresh_rows = lax.all_gather(picked, "blk", axis=3, tiled=True)
    current = tokens
    for pass_index in range(PASSES):
        state_f32 = current.astype(jnp.float32)
        normed = layer_norm(state_f32).astype(jnp.bfloat16)
        projected = jnp.einsum(
            "rbd,dhc->rbhc", normed, w_qkv, preferred_element_type=jnp.float32
        ).astype(jnp.bfloat16)
        head_rows = attend(projected, own_cache, lengths, head_dim)
        partial_terms = jnp.einsum(
            "rbhc,hcd->rbd", head_rows, w_out, preferred_element_type=jnp.float32
        )
        middle = state_f32 + lax.psum(partial_terms.astype(jnp.bfloat16), "blk").astype(jnp.float32)
        normed_mid = layer_norm(middle).astype(jnp.bfloat16)
        hidden = jax.nn.gelu(
            jnp.einsum("rbd,df->rbf", normed_mid, w_fc, preferred_element_type=jnp.float32),
            approximate=True,
        ).astype(jnp.bfloat16)
        grown_rows = jnp.einsum("rbf,fd->rbd", hidden, w_proj, preferred_element_type=jnp.float32)
        current = (
            middle + lax.psum(grown_rows.astype(jnp.bfloat16), "blk").astype(jnp.float32)
        ).astype(jnp.bfloat16)
        current = jnp.where(accept[pass_index][..., None] == 1, fresh_rows[pass_index], current)
    return current


def solution(mesh):
    return jax.shard_map(
        shards,
        mesh=mesh,
        in_specs=(
            P("req", None, None),
            P(None, "req", "blk", None),
            P(None, "blk", None),
            P("blk", None, None),
            P(None, "blk"),
            P("blk", None),
            P("req", "blk"),
            P(),
            P(),
            P(None, "req", None),
            P(),
        ),
        out_specs=P("req", None, None),
        check_vma=False,
    )
```

profile of v0, /device:TPU:6, one launch (start us, length us, event | category | flops | bytes accessed | tf_op | source)
XLA Modules:
  0.0 969.9 jit_solution(16571325852743032627)
XLA Ops:
  9.8 57.4 %gather_fusion = bf16[16384,100]{1,0:T(8,128)(2,1)} fusion(bf16[3141,100]{1,0:T(8,128)(2,1)S(1)} %copy.29, s32[16384]{0:T(1024)S(1)} %broadcast_clamp_fusion), kind=kCustom, calls=%fused_computation | custom fusion | bytes 6619136 | tf_op jit(solution)/shard_map/jit(_take)/gather | solution.py:85
  67.2 7.7 copy.44
  74.9 2.3 select_select_fusion
  77.2 5.1 copy.31
  86.8 2.7 all-gather.5.cloned.1.call-done
  89.6 5.7 slice_bitcast_fusion.1
  95.3 4.4 gather_fusion.3
  99.6 4.3 gather_fusion.2
  103.9 4.0 maximum_select_fusion
  107.9 6.4 copy.37
  114.4 34.5 %while.34 = (s32[]{:T(128)}, f32[2,1,256]{2,0,1:T(2,128)S(1)}, f32[2,1,256]{2,0,1:T(2,128)S(1)}, f32[2,1,256,64]{2,3,0,1:T(8,128)S(1)}, s32[2]{0:T(128)S(1)}, /*...) while((s32[]{:T(128)}, f32[2,1,256]{2,0,1:T(2,128)S(1)}, ...), condition=%wide.region_8.9_spmd, body=%wide.region_5.8_spmd.sunk | while | flops 140055040 | bytes 7192775 | solution.py:64
  152.0 92.6 %all-reduce.15.cloned.1.call-done = bf16[2,32,256,100]{2,0,3,1:T(2,128)(2,1)} async-done(((bf16[2,32,256,100]{2,0,3,1:T(2,128)(2,1)}), bf16[2,32,256,100]{2,0,3,1:T(2,128)(2,1)}) %all-reduce.15.cloned.1.call-update) | async-done | bytes 3276816
  246.8 147.8 %all-reduce.7.cloned.1.call-done = bf16[2,256,1600]{1,2,0:T(8,128)(2,1)} async-done(((bf16[2,256,1600]{1,2,0:T(8,128)(2,1)}), bf16[2,256,1600]{1,2,0:T(8,128)(2,1)}) %all-reduce.7.cloned.1.call-update) | async-done | bytes 1638416 | tf_op jit(solution)/shard_map/psum | solution.py:104
  397.3 5.1 convolution_convert_fusion.3
  402.5 75.9 %all-gather.3.cloned.1.call-done = bf16[2,2,256,1600]{2,1,0,3:T(2,128)(2,1)} async-done(((bf16[2,2,256,100]{2,1,0,3:T(2,128)(2,1)}), bf16[2,2,256,1600]{2,1,0,3:T(2,128)(2,1)}) %all-gather.3.cloned.1.call-update) | async-done | bytes 3276816 | tf_op jit(solution)/shard_map/all_gather | solution.py:92
  478.4 5.4 fusion.135
  483.8 139.8 %all-reduce.9.cloned.1.call-done = bf16[2,256,1600]{1,2,0:T(8,128)(2,1)} async-done(((bf16[2,256,1600]{1,2,0:T(8,128)(2,1)}), bf16[2,256,1600]{1,2,0:T(8,128)(2,1)}) %all-reduce.9.cloned.1.call-update) | async-done | bytes 1638416 | tf_op jit(solution)/shard_map/psum | solution.py:112
  623.6 3.4 convert_reduce_fusion
  628.8 34.4 %while.35 = (s32[]{:T(128)}, f32[2,1,256]{2,0,1:T(2,128)S(1)}, f32[2,1,256]{2,0,1:T(2,128)S(1)}, f32[2,1,256,64]{2,3,0,1:T(8,128)S(1)}, s32[2]{0:T(128)S(1)}, /*...) while((s32[]{:T(128)}, f32[2,1,256]{2,0,1:T(2,128)S(1)}, ...), condition=%wide.region_20.21_spmd, body=%wide.region_17.20_spmd.sunk | while | flops 140055040 | bytes 7192775 | solution.py:64
  665.4 142.6 %all-reduce.11.cloned.1.call-done = bf16[2,256,1600]{1,2,0:T(8,128)(2,1)} async-done(((bf16[2,256,1600]{1,2,0:T(8,128)(2,1)}), bf16[2,256,1600]{1,2,0:T(8,128)(2,1)}) %all-reduce.11.cloned.1.call-update) | async-done | bytes 1638416 | tf_op jit(solution)/shard_map/psum | solution.py:104
  808.0 2.0 fusion.39
  810.6 5.1 convolution_convert_fusion.2
  815.8 142.9 %all-reduce.13.cloned.1.call-done = bf16[2,256,1600]{1,2,0:T(8,128)(2,1)} async-done(((bf16[2,256,1600]{1,2,0:T(8,128)(2,1)}), bf16[2,256,1600]{1,2,0:T(8,128)(2,1)}) %all-reduce.13.cloned.1.call-update) | async-done | bytes 1638416 | tf_op jit(solution)/shard_map/psum | solution.py:112
  958.7 4.4 fusion.43
  (209 shorter events, 87.5 us)
Async XLA Ops:
  6.5 390.8 %copy-start = (bf16[400,1600]{1,0:T(8,128)(2,1)S(1)}, bf16[400,1600]{1,0:T(8,128)(2,1)}, u32[]{:S(2)}) copy-start(bf16[400,1600]{1,0:T(8,128)(2,1)} %param.20) | copy-start | bytes 3840004
  6.5 83.0 %all-gather.5.cloned.1.call-start = ((), (), s32[]{:S(2)}) async-start(), calls=%async_computation.1 | async-start | bytes 8912896 | tf_op jit(solution)/shard_map/all_gather | solution.py:79
  7.3 237.3 %all-reduce.15.cloned.1.call-start = ((), (), s32[]{:S(2)}) async-start(), calls=%async_computation.6 | async-start | bytes 6553600
  82.3 1.4 copy-start.2
  82.3 312.3 %all-reduce.7.cloned.1.call-start = ((), (), s32[]{:S(2)}) async-start(), calls=%async_computation.2 | async-start | bytes 3276800 | tf_op jit(solution)/shard_map/psum | solution.py:104
  83.7 1.1 copy-start.11
  84.8 1.3 copy-start.10
  84.8 1.4 copy-start.1
  85.5 9.8 %copy-start.7 = (bf16[2,256,1,192]{1,3,0,2:T(8,128)(2,1)}, bf16[2,256,1,192]{1,3,0,2:T(8,128)(2,1)S(1)}, u32[]{:S(2)}) copy-start(bf16[2,256,1,192]{1,3,0,2:T(8,128)(2,1)S(1)} %fusion.66) | copy-start | bytes 589828
  107.9 6.4 slice-start
  114.4 34.5 %copy-start.8 = (bf16[1,64,1600]{2,1,0:T(8,128)(2,1)S(1)}, bf16[1,64,1600]{2,1,0:T(8,128)(2,1)}, u32[]{:S(2)}) copy-start(bf16[1,64,1600]{2,1,0:T(8,128)(2,1)} %param.18) | copy-start | bytes 614404
  148.9 1.9 copy-start.13
  150.7 327.7 %all-gather.3.cloned.1.call-start = ((), (), s32[]{:S(2)}) async-start(), calls=%async_computation | async-start | bytes 3481600 | tf_op jit(solution)/shard_map/all_gather | solution.py:92
  246.6 377.0 %all-reduce.9.cloned.1.call-start = ((), (), s32[]{:S(2)}) async-start(), calls=%async_computation.3 | async-start | bytes 3276800 | tf_op jit(solution)/shard_map/psum | solution.py:112
  394.6 2.0 copy-start.5
  397.3 5.2 copy-start.9
  402.5 405.5 %all-reduce.11.cloned.1.call-start = ((), (), s32[]{:S(2)}) async-start(), calls=%async_computation.4 | async-start | bytes 3276800 | tf_op jit(solution)/shard_map/psum | solution.py:104
  623.6 3.9 copy-start.12
  627.0 1.2 copy-start.3
  663.2 144.7 %copy-start.4 = (bf16[2,256,1600]{1,2,0:T(8,128)(2,1)S(1)}, bf16[2,256,1600]{1,2,0:T(8,128)(2,1)}, u32[]{:S(2)}) copy-start(bf16[2,256,1600]{1,2,0:T(8,128)(2,1)} %copy-done.3) | copy-start | bytes 4915204
  665.1 293.6 %all-reduce.13.cloned.1.call-start = ((), (), s32[]{:S(2)}) async-start(), calls=%async_computation.5 | async-start | bytes 3276800 | tf_op jit(solution)/shard_map/psum | solution.py:112
  808.0 2.0 copy-start.6
Sparse Core Ops, SparseCore 0:
  10.1 79.3 all-gather.4
  92.2 152.3 all-reduce.14
  247.3 147.2 all-reduce.6
  396.4 81.9 all-gather.2
  481.1 142.4 all-reduce.8
  665.2 142.7 all-reduce.10
  815.9 142.7 all-reduce.12
where the time goes:
time: 971 us; the launch traced here: 970 us
  waiting for transfers between devices  745 us (77%)
  local copies, waits for them, and re-layouts  103 us (11%)
  matrix products  72.2 us (7%)
  other arithmetic  33.6 us (3%)
  between operations  14.4 us (1%)
    psum x2, waiting for transfers between devices, shards(): lax.psum(partial_terms.astype(jnp.bfloat16), 'blk').astype(jnp.float32)  290 us
    psum x2, waiting for transfers between devices, shards(): lax.psum(grown_rows.astype(jnp.bfloat16), 'blk').astype(jnp.float32)  283 us
    unnamed x8, waiting for transfers between devices  93.4 us
    all_gather x1, waiting for transfers between devices, shards(): fresh_rows = lax.all_gather(picked, 'blk', axis=3, tiled=True)  75.9 us
    gather x2, local copies, waits for them, and re-layouts, shards(): looked = jnp.take(embed_table, jnp.clip(relative, 0, vocab_dev - 1), axis=0)  65.1 us
    dot_general x16, matrix products, visit_block(): jnp.einsum('rhqk,rkhd->rhqd', weights_raw.astype(jnp.bfloat16), cache_pie...  29.2 us
    dot_general x16, matrix products, visit_block(): jnp.einsum('rqhd,rkhd->rhqk', queries, cache_piece[..., :head_dim], prefe...  26.9 us
  transfers between devices with their start and end apart: 7, of which 7 were waited for; matrix products, arithmetic and copies ran while one was open for 16% of the time, Pallas kernels for 0%

commit v1 on v0

--- a/solution.py
+++ b/solution.py
@@ -89,7 +89,9 @@
         .astype(jnp.float32)
         .astype(jnp.bfloat16)
     )
-    fresh_rows = lax.all_gather(picked, "blk", axis=3, tiled=True)
+    fresh_rows = jnp.concatenate(
+        lax.all_to_all(jnp.stack([picked] * lax.axis_size("blk")), "blk", 0, 0), axis=3
+    )
     current = tokens
     for pass_index in range(PASSES):
         state_f32 = current.astype(jnp.float32)

time: 971 us -> 1050 us (1.081)
  waiting for transfers between devices: 745 us -> 813 us
    all_gather x1, waiting for transfers between devices: 2.73 us -> 97.5 us  [shards(): every_cache = lax.all_gather(cache_kv, 'req', axis=1, tiled=True)]
    all_gather x1 -> x0, waiting for transfers between devices: 75.9 us -> none  [shards(): fresh_rows = lax.all_gather(picked, 'blk', axis=3, tiled=True)]
    unnamed x8 -> x7, waiting for transfers between devices: 93.4 us -> 151 us
  transfers between devices with their start and end apart: 7 -> 7, of which waited for: 7 -> 6; matrix products, arithmetic and copies ran while one was open for 16% -> 8% of each run, Pallas kernels for 0% -> 0%
where the time goes in v1:
time: 1050 us
  waiting for transfers between devices  813 us (77%)
  local copies, waits for them, and re-layouts  103 us (10%)
  matrix products  72.2 us (7%)
  other arithmetic  38.2 us (4%)
  between operations  14.5 us (1%)
    psum x2, waiting for transfers between devices, shards(): lax.psum(partial_terms.astype(jnp.bfloat16), 'blk').astype(jnp.float32)  286 us
    psum x2, waiting for transfers between devices, shards(): lax.psum(grown_rows.astype(jnp.bfloat16), 'blk').astype(jnp.float32)  279 us
    unnamed x7, waiting for transfers between devices  151 us
    all_gather x1, waiting for transfers between devices, shards(): every_cache = lax.all_gather(cache_kv, 'req', axis=1, tiled=True)  97.5 us
    gather x2, local copies, waits for them, and re-layouts, shards(): looked = jnp.take(embed_table, jnp.clip(relative, 0, vocab_dev - 1), axis=0)  67.8 us
    dot_general x16, matrix products, visit_block(): jnp.einsum('rhqk,rkhd->rhqd', weights_raw.astype(jnp.bfloat16), cache_pie...  29.2 us
    dot_general x16, matrix products, visit_block(): jnp.einsum('rqhd,rkhd->rhqk', queries, cache_piece[..., :head_dim], prefe...  26.9 us
  transfers between devices with their start and end apart: 7, of which 6 were waited for; matrix products, arithmetic and copies ran while one was open for 8% of the time, Pallas kernels for 0%

profile of v1, /device:TPU:6, one launch (start us, length us, event | category | flops | bytes accessed | tf_op | source)
XLA Modules:
  0.0 1051.6 jit_solution(1464876640381743888)
XLA Ops:
  9.2 57.4 %gather_fusion = bf16[16384,100]{1,0:T(8,128)(2,1)} fusion(bf16[3141,100]{1,0:T(8,128)(2,1)S(1)} %copy.31, s32[16384]{0:T(1024)S(1)} %broadcast_clamp_fusion), kind=kCustom, calls=%fused_computation | custom fusion | bytes 6619136 | tf_op jit(solution)/shard_map/jit(_take)/gather | solution.py:85
  66.7 10.4 copy.32
  77.0 6.9 broadcast_select_fusion.1
  89.8 149.8 %all-reduce.15.cloned.1.call-done = bf16[2,32,256,100]{2,0,3,1:T(2,128)(2,1)} async-done(((bf16[2,32,256,100]{2,0,3,1:T(2,128)(2,1)}), bf16[2,32,256,100]{2,0,3,1:T(2,128)(2,1)}) %all-reduce.15.cloned.1.call-update) | async-done | bytes 3276816
  240.9 3.4 stack.2
  244.3 8.5 all-to-all-start
  253.0 97.5 %all-gather.2.cloned.1.call-done = bf16[4,8192,1,128]{3,1,0,2:T(8,128)(2,1)} async-done(((bf16[4,512,1,128]{3,1,0,2:T(8,128)(2,1)}), bf16[4,8192,1,128]{3,1,0,2:T(8,128)(2,1)}) %all-gather.2.cloned.1.call-update) | async-done | bytes 8388624 | tf_op jit(solution)/shard_map/all_gather | solution.py:79
  350.5 5.7 slice_bitcast_fusion.1
  356.2 4.4 gather_fusion.3
  360.5 4.3 gather_fusion.2
  364.8 4.0 maximum_select_fusion
  368.8 6.4 copy.38
  375.2 34.5 %while.34 = (s32[]{:T(128)}, f32[2,1,256]{2,0,1:T(2,128)S(1)}, f32[2,1,256]{2,0,1:T(2,128)S(1)}, f32[2,1,256,64]{2,3,0,1:T(8,128)S(1)}, s32[2]{0:T(128)S(1)}, /*...) while((s32[]{:T(128)}, f32[2,1,256]{2,0,1:T(2,128)S(1)}, ...), condition=%wide.region_8.9_spmd, body=%wide.region_5.8_spmd.sunk | while | flops 140055040 | bytes 7192775 | solution.py:64
  411.6 143.0 %all-reduce.7.cloned.1.call-done = bf16[2,256,1600]{1,2,0:T(8,128)(2,1)} async-done(((bf16[2,256,1600]{1,2,0:T(8,128)(2,1)}), bf16[2,256,1600]{1,2,0:T(8,128)(2,1)}) %all-reduce.7.cloned.1.call-update) | async-done | bytes 1638416 | tf_op jit(solution)/shard_map/psum | solution.py:106
  557.3 5.1 convolution_convert_fusion.3
  562.8 5.9 fusion.135
  568.7 136.4 %all-reduce.9.cloned.1.call-done = bf16[2,256,1600]{1,2,0:T(8,128)(2,1)} async-done(((bf16[2,256,1600]{1,2,0:T(8,128)(2,1)}), bf16[2,256,1600]{1,2,0:T(8,128)(2,1)}) %all-reduce.9.cloned.1.call-update) | async-done | bytes 1638416 | tf_op jit(solution)/shard_map/psum | solution.py:114
  705.2 3.4 convert_reduce_fusion
  710.4 34.5 %while.35 = (s32[]{:T(128)}, f32[2,1,256]{2,0,1:T(2,128)S(1)}, f32[2,1,256]{2,0,1:T(2,128)S(1)}, f32[2,1,256,64]{2,3,0,1:T(8,128)S(1)}, s32[2]{0:T(128)S(1)}, /*...) while((s32[]{:T(128)}, f32[2,1,256]{2,0,1:T(2,128)S(1)}, ...), condition=%wide.region_20.21_spmd, body=%wide.region_17.20_spmd.sunk | while | flops 140055040 | bytes 7192775 | solution.py:64
  746.7 142.9 %all-reduce.11.cloned.1.call-done = bf16[2,256,1600]{1,2,0:T(8,128)(2,1)} async-done(((bf16[2,256,1600]{1,2,0:T(8,128)(2,1)}), bf16[2,256,1600]{1,2,0:T(8,128)(2,1)}) %all-reduce.11.cloned.1.call-update) | async-done | bytes 1638416 | tf_op jit(solution)/shard_map/psum | solution.py:106
  889.6 2.0 fusion.39
  892.3 5.1 convolution_convert_fusion.2
  897.5 142.9 %all-reduce.13.cloned.1.call-done = bf16[2,256,1600]{1,2,0:T(8,128)(2,1)} async-done(((bf16[2,256,1600]{1,2,0:T(8,128)(2,1)}), bf16[2,256,1600]{1,2,0:T(8,128)(2,1)}) %all-reduce.13.cloned.1.call-update) | async-done | bytes 1638416 | tf_op jit(solution)/shard_map/psum | solution.py:114
  1040.3 4.4 fusion.43
  (210 shorter events, 86.2 us)
Async XLA Ops:
  6.5 550.8 %copy-start = (bf16[400,1600]{1,0:T(8,128)(2,1)S(1)}, bf16[400,1600]{1,0:T(8,128)(2,1)}, u32[]{:S(2)}) copy-start(bf16[400,1600]{1,0:T(8,128)(2,1)} %param.20) | copy-start | bytes 3840004
  6.5 233.1 %all-reduce.15.cloned.1.call-start = ((), (), s32[]{:S(2)}) async-start(), calls=%async_computation.6 | async-start | bytes 6553600
  83.9 1.4 copy-start.2
  83.9 266.5 %all-gather.2.cloned.1.call-start = ((), (), s32[]{:S(2)}) async-start(), calls=%async_computation.1 | async-start | bytes 8912896 | tf_op jit(solution)/shard_map/all_gather | solution.py:79
  85.3 1.1 copy-start.11
  86.0 1.0 copy-start.13
  86.0 2.4 copy-start.10
  86.1 2.5 copy-start.1
  87.1 157.2 %copy-start.7 = (bf16[2,256,1,192]{1,3,0,2:T(8,128)(2,1)}, bf16[2,256,1,192]{1,3,0,2:T(8,128)(2,1)S(1)}, u32[]{:S(2)}) copy-start(bf16[2,256,1,192]{1,3,0,2:T(8,128)(2,1)S(1)} %fusion.66) | copy-start | bytes 589828
  244.3 318.5 %all-to-all-start = ((bf16[16,2,2,256,100]{3,2,4,1,0:T(2,128)(2,1)}), bf16[16,2,2,256,100]{3,2,4,1,0:T(2,128)(2,1)}, u32[]{:S(2)}, u32[]{:S(2)}) async-start(bf16[16,2,2,256,100]{3,2,4,1,0:T(2,128)(2,1)} %stack.2), calls=%async_computation | async-start | bytes 6553600 | tf_op jit(solution)/shard_map/all_to_all | solution.py:93
  252.8 301.9 %all-reduce.7.cloned.1.call-start = ((), (), s32[]{:S(2)}) async-start(), calls=%async_computation.2 | async-start | bytes 3276800 | tf_op jit(solution)/shard_map/psum | solution.py:106
  368.8 6.4 slice-start
  375.2 34.5 %copy-start.8 = (bf16[1,64,1600]{2,1,0:T(8,128)(2,1)S(1)}, bf16[1,64,1600]{2,1,0:T(8,128)(2,1)}, u32[]{:S(2)}) copy-start(bf16[1,64,1600]{2,1,0:T(8,128)(2,1)} %param.18) | copy-start | bytes 614404
  411.5 293.6 %all-reduce.9.cloned.1.call-start = ((), (), s32[]{:S(2)}) async-start(), calls=%async_computation.3 | async-start | bytes 3276800 | tf_op jit(solution)/shard_map/psum | solution.py:114
  554.6 2.0 copy-start.5
  557.3 5.4 copy-start.9
  562.5 327.1 %all-reduce.11.cloned.1.call-start = ((), (), s32[]{:S(2)}) async-start(), calls=%async_computation.4 | async-start | bytes 3276800 | tf_op jit(solution)/shard_map/psum | solution.py:106
  705.2 3.9 copy-start.12
  708.6 1.2 copy-start.3
  744.8 144.8 %copy-start.4 = (bf16[2,256,1600]{1,2,0:T(8,128)(2,1)S(1)}, bf16[2,256,1600]{1,2,0:T(8,128)(2,1)}, u32[]{:S(2)}) copy-start(bf16[2,256,1600]{1,2,0:T(8,128)(2,1)} %copy-done.3) | copy-start | bytes 4915204
  746.7 293.6 %all-reduce.13.cloned.1.call-start = ((), (), s32[]{:S(2)}) async-start(), calls=%async_computation.5 | async-start | bytes 3276800 | tf_op jit(solution)/shard_map/psum | solution.py:114
  889.6 2.0 copy-start.6
Sparse Core Ops, SparseCore 0:
  84.0 155.5 all-reduce.14
  242.4 108.0 all-gather.1
  411.7 142.9 all-reduce.6
  562.6 142.5 all-reduce.8
  746.8 142.7 all-reduce.10
  897.6 142.6 all-reduce.12
